TPU v7x, 32 devices: a whole 2x2x4 slice. The times are simulated.
32 devices in a mesh: ha: 4 (over z), wa: 2 (over y), ba: 4 (over x, core).
Axes of the slice: x: 2, y: 2, z: 4, core: 2. Of those that a mesh axis runs over, the one named last changes fastest.
Arguments:
- tokens: bfloat16 [32, 32, 16, 512], P('ba', 'ha', 'wa'), parts along dimension 0, may hold values from -6 to 6
- norm_gain: float32 [3, 512], replicated, may hold values from 0.1 to 1.9
- w_gatevals: bfloat16 [3, 512, 2048], replicated, may hold values from -0.25 to 0.25
- w_coupling: bfloat16 [3, 512, 128], replicated, may hold values from -0.25 to 0.25
- w_steps: bfloat16 [3, 512, 16], replicated, may hold values from -0.25 to 0.25
- conv_values: float32 [3, 4, 1024], replicated, may hold values from -3 to 3
- conv_coupling: float32 [3, 4, 128], replicated, may hold values from -3 to 3
- step_bias: float32 [3, 16], replicated, may hold values from -4 to 0
- rate_log: float32 [3, 16], replicated, may hold values from -1.5 to 1.5
- skip_gain: float32 [3, 16], replicated, may hold values from 0.5 to 2
- out_gain: float32 [3, 1024], replicated, may hold values from 0.1 to 1.9
- w_output: bfloat16 [3, 1024, 512], replicated, may hold values from -0.1875 to 0.1875
Outputs:
- result: bfloat16 [32, 32, 16, 512], P('ba', 'ha', 'wa'), parts along dimension 0
There are 4 independent parts, one for each index of `ba`. A program takes and returns all parts, laid end to end along the dimension named above; an argument that names none is the same for every part. Nothing has to cross between parts.
All inputs are finite; a program needn't handle non-finite values.
Results may differ from a plain program's by a relative error of at most 0.025.
Values may be sent and summed in bfloat16 or wider, within the bound.
A program may use at most 128 MiB of HBM per device.

v0:
```python
import functools
import jax
import jax.numpy as jnp
from jax import lax
from jax.experimental import pallas as pl
from jax.experimental.pallas import tpu as pltpu
from jax.sharding import PartitionSpec as P


def causal_conv(values, kernel):
    length = values.shape[1]
    taps = kernel.shape[0]
    padded = jnp.pad(values, ((0, 0), (taps - 1, 0), (0, 0)))
    total = jnp.zeros_like(values)
    for offset in range(taps):
        total = total + padded[:, offset : offset + length, :] * kernel[offset]
    return total


def mixer(stream, params):
    (
        norm_gain,
        w_gatevals,
        w_coupling,
        w_steps,
        conv_values,
        conv_coupling,
        step_bias,
        rate_log,
        skip_gain,
        out_gain,
        w_output,
    ) = params
    count, length, width = stream.shape
    inner = w_gatevals.shape[1] // 2
    states = w_coupling.shape[1] // 2
    heads = w_steps.shape[1]
    headdim = inner // heads
    flat = stream.reshape(count * length, width).astype(jnp.float32)
    normed = (
        flat * lax.rsqrt(jnp.mean(flat * flat, axis=-1, keepdims=True) + 1e-05) * norm_gain
    ).astype(jnp.bfloat16)
    gatevals = jnp.dot(normed, w_gatevals, preferred_element_type=jnp.float32).astype(jnp.bfloat16)
    coupling = jnp.dot(normed, w_coupling, preferred_element_type=jnp.float32).astype(jnp.bfloat16)
    step_raw = jnp.dot(normed, w_steps, preferred_element_type=jnp.float32)
    gate = gatevals[:, :inner]
    values = gatevals[:, inner:]
    xs = jax.nn.silu(
        causal_conv(values.astype(jnp.float32).reshape(count, length, inner), conv_values)
    ).astype(jnp.bfloat16)
    maps = jax.nn.silu(
        causal_conv(coupling.astype(jnp.float32).reshape(count, length, 2 * states), conv_coupling)
    ).astype(jnp.bfloat16)
    input_map = maps[:, :, :states]
    output_map = maps[:, :, states:]
    steps = jax.nn.softplus(step_raw.reshape(count, length, heads) + step_bias)
    cumul = jnp.cumsum(steps * -jnp.exp(rate_log), axis=1).transpose(0, 2, 1)
    steps_heads = steps.transpose(0, 2, 1)
    positions = jnp.arange(length, dtype=jnp.int32)
    lower = positions[:, None] >= positions[None, :]
    spread = cumul[:, :, :, None] - cumul[:, :, None, :]
    decay = jnp.exp(jnp.where(lower[None, None, :, :], spread, -jnp.inf))
    scores = jnp.einsum("ntk,nsk->nts", output_map, input_map, preferred_element_type=jnp.float32)
    weights = (scores[:, None, :, :] * decay * steps_heads[:, :, None, :]).astype(jnp.bfloat16)
    heads_in = xs.reshape(count, length, heads, headdim)
    mixed = jnp.einsum("nhts,nshp->nthp", weights, heads_in, preferred_element_type=jnp.float32)
    mixed = mixed + skip_gain[:, None] * heads_in.astype(jnp.float32)
    gated = mixed.reshape(count * length, inner) * jax.nn.silu(gate.astype(jnp.float32))
    normal = (
        gated * lax.rsqrt(jnp.mean(gated * gated, axis=-1, keepdims=True) + 1e-05) * out_gain
    ).astype(jnp.bfloat16)
    update = jnp.dot(normal, w_output, preferred_element_type=jnp.float32)
    return (flat + update).astype(jnp.bfloat16).reshape(count, length, width)


def shards_general(
    tokens,
    norm_gain,
    w_gatevals,
    w_coupling,
    w_steps,
    conv_values,
    conv_coupling,
    step_bias,
    rate_log,
    skip_gain,
    out_gain,
    w_output,
):
    stacked = (
        norm_gain,
        w_gatevals,
        w_coupling,
        w_steps,
        conv_values,
        conv_coupling,
        step_bias,
        rate_log,
        skip_gain,
        out_gain,
        w_output,
    )

    def params_of(index):
        return tuple((member[index] for member in stacked))

    frames, rows_dev, cols_dev, width = tokens.shape
    height_devs = lax.axis_size("ha")
    width_devs = lax.axis_size("wa")
    streams = tokens.transpose(1, 2, 0, 3).reshape(rows_dev * cols_dev, frames, width)
    current = (
        mixer(streams, params_of(0))
        .reshape(rows_dev, cols_dev, frames, width)
        .transpose(2, 0, 1, 3)
    )
    piece = lax.all_to_all(current, "ha", split_axis=0, concat_axis=1, tiled=True)
    frame_part, rows_all, col_count, _ = piece.shape
    streams = piece.transpose(0, 2, 1, 3).reshape(frame_part * col_count, rows_all, width)
    output = mixer(streams, params_of(1))
    current = output.reshape(frame_part, col_count, rows_all, width).transpose(0, 2, 1, 3)
    frame_part = current.shape[0]
    rows_all = current.shape[1]
    split_rows = current.reshape(frame_part, rows_all // width_devs, width_devs, cols_dev, width)
    piece = lax.all_to_all(split_rows, "wa", split_axis=2, concat_axis=3, tiled=True)
    part_frames, row_count, single, cols_all, _ = piece.shape
    streams = piece.reshape(part_frames * row_count * single, cols_all, width)
    output = mixer(streams, params_of(2))
    current = output.reshape(part_frames, row_count, single, cols_all, width)
    row_group = rows_dev // width_devs
    arranged = current.reshape(frame_part, height_devs, row_group, width_devs, cols_dev, width)
    arranged = arranged.transpose(1, 3, 0, 2, 4, 5).reshape(
        height_devs * width_devs, frame_part, row_group, cols_dev, width
    )
    received = lax.all_to_all(arranged, ("ha", "wa"), split_axis=0, concat_axis=0, tiled=True)
    received = received.reshape(height_devs, width_devs, frame_part, row_group, cols_dev, width)
    result = received.transpose(0, 2, 3, 1, 4, 5).reshape(frames, rows_dev, cols_dev, width)
    return result


ROWS = 128
F32 = jnp.float32
BF16 = jnp.bfloat16
MESH = pl.DeviceIdType.MESH


def silu(x):
    half = 0.5 * x
    return half + half * jnp.tanh(half)


def rounded(x):
    return x.astype(BF16).astype(F32)


def project(layer, x, refs, n_block, store, wait=None):
    wg, wc, ws, ng = refs
    scale = lax.rsqrt(jnp.mean(x * x, axis=-1, keepdims=True) + 1e-05)
    normed = (x * scale * ng[layer : layer + 1, :]).astype(BF16)
    coupling = rounded(jnp.dot(normed, wc[layer], preferred_element_type=F32))
    steps = jnp.dot(normed, ws[layer], preferred_element_type=F32)
    store(None, (coupling, steps))
    total = wg.shape[2]
    for first in range(0, total, n_block):
        if wait is not None:
            wait(first // n_block)
        block = jnp.dot(normed, wg[layer, :, first : first + n_block], preferred_element_type=F32)
        store(first, rounded(block))


def mix(layer, length, stride, gate_of, value_of, coupling, steps, x, params, gated, normal):
    cv, cc, sb, rl, sk, og, wo = params
    rows = coupling.shape[0]
    heads = sb.shape[1]
    inner = cv.shape[2]
    headdim = inner // heads
    taps = cv.shape[1]
    states = coupling.shape[1] // 2
    i = lax.broadcasted_iota(jnp.int32, (rows, rows), 0)
    j = lax.broadcasted_iota(jnp.int32, (rows, rows), 1)
    if stride == 1:
        same = (i // length) == (j // length)
    else:
        same = (i % stride) == (j % stride)
    mask = same & (i >= j)

    def shift(v, by):
        if stride == 1:
            position = lax.broadcasted_iota(jnp.int32, v.shape, 0) % length
            return jnp.where(position >= by, pltpu.roll(v, by, 0), 0.0)
        pad = jnp.zeros((by * stride, v.shape[1]), v.dtype)
        return jnp.concatenate([pad, v[: rows - by * stride]], axis=0)

    def conv(v, kernel):
        total = v * kernel[taps - 1 : taps]
        for back in range(1, taps):
            total = total + shift(v, back) * kernel[taps - 1 - back : taps - back]
        return silu(total)

    maps = conv(coupling, cc[layer]).astype(BF16)
    scores = lax.dot_general(
        maps[:, states:], maps[:, :states], (((1,), (1,)), ((), ())), preferred_element_type=F32
    )
    raw = steps + sb[layer : layer + 1, :]
    steps = jnp.maximum(raw, 0.0) + jnp.log1p(jnp.exp(-jnp.abs(raw)))
    cumul = steps * -jnp.exp(rl[layer : layer + 1, :])
    by = 1
    while by < length:
        cumul = cumul + shift(cumul, by)
        by *= 2
    cumul_t = cumul.T
    steps_t = steps.T
    pair = 2 * headdim
    lane = lax.broadcasted_iota(jnp.int32, (1, pair), 1)
    squares = jnp.zeros((rows, pair), F32)
    for p in range(heads // 2):
        lanes = slice(p * pair, (p + 1) * pair)
        xs = conv(value_of(lanes), cv[layer, :, lanes]).astype(BF16).astype(F32)
        weights = []
        for h in (2 * p, 2 * p + 1):
            spread = cumul[:, h : h + 1] - cumul_t[h : h + 1, :]
            decay = jnp.exp(jnp.where(mask, spread, -jnp.inf))
            weights.append((scores * decay * steps_t[h : h + 1, :]).astype(BF16))
        both = jnp.concatenate(
            [jnp.where(lane < headdim, xs, 0.0), jnp.where(lane < headdim, 0.0, xs)], axis=0
        ).astype(BF16)
        mixed = jnp.dot(jnp.concatenate(weights, axis=1), both, preferred_element_type=F32)
        skip = jnp.where(
            lane < headdim,
            sk[layer : layer + 1, 2 * p : 2 * p + 1],
            sk[layer : layer + 1, 2 * p + 1 : 2 * p + 2],
        )
        part = (mixed + skip * xs) * silu(gate_of(lanes))
        squares = squares + part * part
        gated[:, lanes] = part
    scale = lax.rsqrt(jnp.sum(squares, axis=-1, keepdims=True) / inner + 1e-05)
    for p in range(heads // 2):
        lanes = slice(p * pair, (p + 1) * pair)
        normal[:, lanes] = (gated[:, lanes] * scale * og[layer : layer + 1, lanes]).astype(BF16)
    return x + jnp.dot(normal[...], wo[layer], preferred_element_type=F32)


def swap_matrix(outer, first, second):
    n = outer * first * second
    i = lax.broadcasted_iota(jnp.int32, (n, n), 0)
    j = lax.broadcasted_iota(jnp.int32, (n, n), 1)
    o, a, b = i // (first * second), (i // second) % first, i % second
    return jnp.where(o * first * second + b * first + a == j, 1.0, 0.0).astype(BF16)


def sweeps(
    sizes, tok_hbm, ng, wg_hbm, wc, ws, cv, cc, sb, rl, sk, og, wo_hbm, out,
    tok, wg, wo, x0, gv0, coup0, step0, gv1, x2, gv2, coup2, step2,
    landed, sent, gated, normal, back,
    tok_sem, wg_sem, wo_sem, send1, recv1, send2, recv2,
):
    ha_n, wa_n, frames, rows_dev, cols_dev, width = sizes
    peers = ha_n * wa_n
    cpc = ROWS // (frames * rows_dev)
    chunks = cols_dev // cpc
    rows_all, cols_all = rows_dev * ha_n, cols_dev * wa_n
    tokens = frames * rows_dev * cols_dev
    ha, wa = lax.axis_index("ha"), lax.axis_index("wa")
    me = ha * wa_n + wa
    blocks = wg_sem.shape[1]
    n_block = wg.shape[2] // blocks

    def device(index):
        return {"ha": index // wa_n, "wa": lax.rem(index, wa_n)}

    fetch = pltpu.make_async_copy(tok_hbm, tok, tok_sem)
    fetch.start()
    wg_copies = {}
    wo_copies = []
    layers = wg.shape[0]
    for layer in range(layers):
        for b in range(blocks):
            span = pl.ds(b * n_block, n_block)
            copy = pltpu.make_async_copy(
                wg_hbm.at[layer, :, span], wg.at[layer, :, span], wg_sem.at[layer, b]
            )
            copy.start()
            wg_copies[layer, b] = copy
        copy = pltpu.make_async_copy(wo_hbm.at[layer], wo.at[layer], wo_sem.at[layer])
        copy.start()
        wo_copies.append(copy)

    barrier = pltpu.get_barrier_semaphore()
    for k in range(1, peers):
        pl.semaphore_signal(
            barrier, inc=1, device_id=device(lax.rem(me + k, peers)), device_id_type=MESH
        )

    refs = (wg, wc, ws, ng)
    params = (cv, cc, sb, rl, sk, og, wo)
    inner = cv.shape[2]

    fetch.wait()
    swap = swap_matrix(ROWS // (rows_dev * cols_dev), cols_dev, rows_dev)
    for first in range(0, tokens, ROWS):
        part = tok[...].astype(F32).reshape(tokens, width)[first : first + ROWS].astype(BF16)
        group = ROWS // (rows_dev * cols_dev)
        x0[first // ROWS * group : (first // ROWS + 1) * group] = jnp.dot(
            swap, part, preferred_element_type=F32
        ).reshape(group, rows_dev * cols_dev, width)

    def keep_in(wide, coupling, steps):
        def store(first, value):
            if first is None:
                coupling[...] = value[0].reshape(coupling.shape)
                steps[...] = value[1].reshape(steps.shape)
            else:
                size = value.shape[1]
                wide[:, :, first : first + size] = value.reshape(wide.shape[:2] + (size,))

        return store

    project(
        0, x0[...].reshape(tokens, width), refs, n_block, keep_in(gv0, coup0, step0),
        lambda b: wg_copies[0, b].wait(),
    )
    wo_copies[0].wait()
    pl.semaphore_wait(barrier, peers - 1)

    span = rows_dev * cpc

    def view(ref, c, size):
        return lambda lanes: ref[
            :, pl.ds(pl.multiple_of(c * size, size), size), lanes
        ].reshape(ROWS, -1)

    def out1(c, k):
        peer = lax.rem(me + k, peers)
        return pltpu.make_async_remote_copy(
            src_ref=sent.at[peer, c],
            dst_ref=landed.at[c, wa, :, ha],
            send_sem=send1.at[c, k],
            recv_sem=recv1.at[c, k],
            device_id=device(peer),
            device_id_type=MESH,
        )

    def layer0(c, carry):
        pick = view(gv0, c, span)
        y = mix(
            0, frames, span,
            lambda lanes: pick(lanes),
            lambda lanes: pick(slice(inner + lanes.start, inner + lanes.stop)),
            view(coup0, c, span)(slice(None)), view(step0, c, span)(slice(None)),
            view(x0, c, span)(slice(None)),
            params, gated, normal,
        )
        sent[:, pl.ds(c, 1)] = y.reshape(frames, 1, cpc, rows_dev, width).astype(BF16)
        for k in range(1, peers):
            out1(c, k).start()
        landed[pl.ds(c, 1), pl.ds(wa, 1), :, pl.ds(ha, 1)] = sent[
            pl.ds(me, 1), pl.ds(c, 1)
        ].reshape(1, 1, cpc, 1, rows_dev, width)
        return carry

    lax.fori_loop(0, chunks, layer0, 0)

    for b in range(blocks):
        wg_copies[1, b].wait()
    wo_copies[1].wait()

    def layer1(c, carry):
        for k in range(1, peers):
            out1(c, k).wait_recv()
        x = landed[pl.ds(c, 1)].astype(F32).reshape(ROWS, width)
        held = []

        def store_part(first, value):
            if first is None:
                held.extend(value)
            else:
                gv1[:, first : first + value.shape[1]] = value

        project(1, x, refs, n_block, store_part)
        y = mix(
            1, rows_all, 1,
            lambda lanes: gv1[:, lanes],
            lambda lanes: gv1[:, inner + lanes.start : inner + lanes.stop],
            held[0], held[1], x, params, gated, normal,
        )
        y = rounded(y).reshape(wa_n, cpc, rows_all, width)
        for w in range(wa_n):
            x2[pl.ds(w * cols_dev + c * cpc, cpc)] = y[w]
        return carry

    lax.fori_loop(0, chunks, layer1, 0)

    for b in range(blocks):
        wg_copies[2, b].wait()
    wo_copies[2].wait()
    project(2, x2[...].reshape(tokens, width), refs, n_block, keep_in(gv2, coup2, step2))
    swap2 = swap_matrix(wa_n, rows_dev, cols_dev)

    def out2(j, q):
        peer_ha, peer_wa = lax.rem(ha + j + 1, ha_n), lax.rem(wa + q, wa_n)
        return pltpu.make_async_remote_copy(
            src_ref=back.at[j, peer_wa],
            dst_ref=out.at[me],
            send_sem=send2.at[j, q],
            recv_sem=recv2.at[j, q],
            device_id={"ha": peer_ha, "wa": peer_wa},
            device_id_type=MESH,
        )

    def layer2(j, carry):
        c = lax.rem(ha + j + 1, ha_n)
        pick = view(gv2, c, rows_dev)
        y = mix(
            2, cols_all, rows_dev,
            lambda lanes: pick(lanes),
            lambda lanes: pick(slice(inner + lanes.start, inner + lanes.stop)),
            view(coup2, c, rows_dev)(slice(None)), view(step2, c, rows_dev)(slice(None)),
            view(x2, c, rows_dev)(slice(None)),
            params, gated, normal,
        )
        turned = jnp.dot(swap2, y.astype(BF16), preferred_element_type=F32)
        back[pl.ds(j, 1)] = turned.reshape(1, wa_n, rows_dev, cols_dev, width).astype(BF16)
        for q in range(wa_n):
            if q == 0:
                pl.when(j < ha_n - 1)(lambda: out2(j, 0).start())
            else:
                out2(j, q).start()
        return carry

    lax.fori_loop(0, ha_n, layer2, 0)
    out[pl.ds(me, 1)] = back[ha_n - 1, pl.ds(wa, 1)]
    for j in range(ha_n):
        for q in range(wa_n):
            if j < ha_n - 1 or q > 0:
                out2(j, q).wait()
    for c in range(chunks):
        for k in range(1, peers):
            out1(c, k).wait_send()


def fits(tokens, ha_n, wa_n):
    frames, rows_dev, cols_dev, _ = tokens.shape
    return (
        frames == ha_n * wa_n
        and rows_dev == 8
        and ROWS % (frames * rows_dev) == 0
        and cols_dev % (ROWS // (frames * rows_dev)) == 0
        and (frames * rows_dev * cols_dev) % ROWS == 0
        and ROWS % (rows_dev * cols_dev) == 0
        and cols_dev * wa_n * rows_dev == ROWS
        and wa_n * (ROWS // (frames * rows_dev)) * rows_dev * ha_n == ROWS
    )


def shards(*arrays):
    tokens, ng, wg, wc, ws, cv, cc, sb, rl, sk, og, wo = arrays
    ha_n, wa_n = lax.axis_size("ha"), lax.axis_size("wa")
    if not fits(tokens, ha_n, wa_n):
        return shards_general(*arrays)
    frames, rows_dev, cols_dev, width = tokens.shape
    count = frames * rows_dev * cols_dev
    layers, _, wide = wg.shape
    inner = wide // 2
    cpc = ROWS // (frames * rows_dev)
    chunks = cols_dev // cpc
    blocks = 4
    early = (frames, rows_dev * cols_dev)
    late = (cols_dev * wa_n, rows_dev * ha_n)
    vmem = pl.BlockSpec(memory_space=pltpu.VMEM)
    hbm = pl.BlockSpec(memory_space=pl.ANY)
    sizes = (ha_n, wa_n, frames, rows_dev, cols_dev, width)
    dma = pltpu.SemaphoreType.DMA
    return pl.pallas_call(
        functools.partial(sweeps, sizes),
        out_shape=jax.ShapeDtypeStruct(tokens.shape, BF16),
        in_specs=[hbm, vmem, hbm, vmem, vmem, vmem, vmem, vmem, vmem, vmem, vmem, hbm],
        out_specs=vmem,
        scratch_shapes=[
            pltpu.VMEM(tokens.shape, BF16),
            pltpu.VMEM(wg.shape, BF16),
            pltpu.VMEM(wo.shape, BF16),
            pltpu.VMEM(early + (width,), F32),
            pltpu.VMEM(early + (wide,), F32),
            pltpu.VMEM(early + (wc.shape[2],), F32),
            pltpu.VMEM(early + (ws.shape[2],), F32),
            pltpu.VMEM((ROWS, wide), F32),
            pltpu.VMEM(late + (width,), F32),
            pltpu.VMEM(late + (wide,), F32),
            pltpu.VMEM(late + (wc.shape[2],), F32),
            pltpu.VMEM(late + (ws.shape[2],), F32),
            pltpu.VMEM((chunks, wa_n, cpc, ha_n, rows_dev, width), BF16),
            pltpu.VMEM((frames, chunks, cpc, rows_dev, width), BF16),
            pltpu.VMEM((ROWS, inner), F32),
            pltpu.VMEM((ROWS, inner), BF16),
            pltpu.VMEM((ha_n, wa_n, rows_dev, cols_dev, width), BF16),
            dma(()),
            dma((layers, blocks)),
            dma((layers,)),
            dma((chunks, ha_n * wa_n)),
            dma((chunks, ha_n * wa_n)),
            dma((ha_n, wa_n)),
            dma((ha_n, wa_n)),
        ],
        compiler_params=pltpu.CompilerParams(
            collective_id=0, has_side_effects=True, vmem_limit_bytes=48 * 2**20
        ),
    )(tokens, ng, wg, wc, ws, cv, cc, sb, rl, sk, og, wo)


def solution(mesh):
    in_specs = (P("ba", "ha", "wa", None),) + (P(),) * 11
    out_specs = P("ba", "ha", "wa", None)
    return jax.shard_map(shards, mesh=mesh, in_specs=in_specs, out_specs=out_specs, check_vma=False)
```

profile of v0, /device:TPU:0, one launch (start us, length us, event | category | flops | bytes accessed | tf_op | source)
XLA Modules:
  0.0 49.3 jit_solution(16019510519337876909)
XLA Ops:
  0.0 1.0 %copy.13.ws = bf16[3,512,16]{2,1,0:T(8,128)(2,1)S(1)} copy(bf16[3,512,16]{1,2,0:T(8,128)(2,1)} %param.16) | data formatting | bytes 98304 | tf_op args[4]
  1.0 0.0 copy-start
  1.0 1.9 %copy-done = bf16[3,1024,512]{2,1,0:T(8,128)(2,1)S(1)} copy-done((bf16[3,1024,512]{2,1,0:T(8,128)(2,1)S(1)}, bf16[3,1024,512]{2,1,0:T(8,128)(2,1)}, u32[]{:S(2)}) %copy-start) | copy-done | bytes 3145752
  2.9 0.0 copy-start.1
  2.9 1.0 %copy-done.1 = bf16[8,8,8,512]{3,2,1,0:T(8,128)(2,1)S(1)} copy-done((bf16[8,8,8,512]{3,2,1,0:T(8,128)(2,1)S(1)}, bf16[8,8,8,512]{3,2,1,0:T(8,128)(2,1)}, u32[]{:S(2)}) %copy-start.1) | copy-done | bytes 524312
  4.0 0.0 copy-start.2
  4.0 1.0 %copy-done.2 = bf16[3,512,128]{2,1,0:T(8,128)(2,1)S(1)} copy-done((bf16[3,512,128]{2,1,0:T(8,128)(2,1)S(1)}, bf16[3,512,128]{2,1,0:T(8,128)(2,1)}, u32[]{:S(2)}) %copy-start.2) | copy-done | bytes 393240
  5.0 0.0 copy-start.3
  5.0 0.8 %copy-done.3 = f32[3,4,1024]{2,1,0:T(4,128)S(1)} copy-done((f32[3,4,1024]{2,1,0:T(4,128)S(1)}, f32[3,4,1024]{2,1,0:T(4,128)}, u32[]{:S(2)}) %copy-start.3) | copy-done | bytes 49176
  5.8 0.0 copy-start.4
  5.8 0.7 %copy-done.4 = f32[3,1024]{1,0:T(4,128)S(1)} copy-done((f32[3,1024]{1,0:T(4,128)S(1)}, f32[3,1024]{1,0:T(4,128)}, u32[]{:S(2)}) %copy-start.4) | copy-done | bytes 12312
  6.5 0.0 copy-start.5
  6.5 0.7 %copy-done.5 = f32[3,512]{1,0:T(4,128)S(1)} copy-done((f32[3,512]{1,0:T(4,128)S(1)}, f32[3,512]{1,0:T(4,128)}, u32[]{:S(2)}) %copy-start.5) | copy-done | bytes 6168
  7.2 0.0 copy-start.6
  7.2 0.7 %copy-done.6 = f32[3,4,128]{2,1,0:T(4,128)S(1)} copy-done((f32[3,4,128]{2,1,0:T(4,128)S(1)}, f32[3,4,128]{2,1,0:T(4,128)}, u32[]{:S(2)}) %copy-start.6) | copy-done | bytes 6168
  7.9 0.0 copy-start.7
  7.9 0.7 %copy-done.7 = f32[3,16]{1,0:T(4,128)S(1)} copy-done((f32[3,16]{1,0:T(4,128)S(1)}, f32[3,16]{1,0:T(4,128)}, u32[]{:S(2)}) %copy-start.7) | copy-done | bytes 216
  8.5 0.0 copy-start.8
  8.5 0.7 %copy-done.8 = f32[3,16]{1,0:T(4,128)S(1)} copy-done((f32[3,16]{1,0:T(4,128)S(1)}, f32[3,16]{1,0:T(4,128)}, u32[]{:S(2)}) %copy-start.8) | copy-done | bytes 216
  9.2 0.0 copy-start.9
  9.2 0.7 %copy-done.9 = f32[3,16]{1,0:T(4,128)S(1)} copy-done((f32[3,16]{1,0:T(4,128)S(1)}, f32[3,16]{1,0:T(4,128)}, u32[]{:S(2)}) %copy-start.9) | copy-done | bytes 216
  9.9 38.6 %shard_map.118 = bf16[8,8,8,512]{3,2,1,0:T(8,128)(2,1)S(1)} custom-call(bf16[8,8,8,512]{3,2,1,0:T(8,128)(2,1)S(1)} %copy-done.1, f32[3,512]{1,0:T(4,128)S(1)} %copy-done.5, bf16[3,512,2048]{2,1,0:T(8,128)(2,1)} %wg_hbm.1, bf16[3,512,128]{2,1,0:T(8,128)(2,1)S(1)} %copy-done.2, bf16[3,512,16]{2,1,0:T(8,128)(2,1)S(1)} %copy.13.ws, f32[3,4,1024]{2,1,0:T(4,128)S(1)} %copy-done.3, ...), custom_call_target="tpu_custom_call" | custom-call | tf_op jit(solution)/shard_map/pallas_call | solution.py:472
  48.5 0.8 %copy.15 = bf16[8,8,8,512]{3,2,1,0:T(8,128)(2,1)} copy(bf16[8,8,8,512]{3,2,1,0:T(8,128)(2,1)S(1)} %shard_map.118) | data formatting | bytes 1048576
Async XLA Ops:
  1.0 1.9 %copy-start = (bf16[3,1024,512]{2,1,0:T(8,128)(2,1)S(1)}, bf16[3,1024,512]{2,1,0:T(8,128)(2,1)}, u32[]{:S(2)}) copy-start(bf16[3,1024,512]{2,1,0:T(8,128)(2,1)} %wo_hbm.1) | copy-start | bytes 9437188
  2.9 1.0 %copy-start.1 = (bf16[8,8,8,512]{3,2,1,0:T(8,128)(2,1)S(1)}, bf16[8,8,8,512]{3,2,1,0:T(8,128)(2,1)}, u32[]{:S(2)}) copy-start(bf16[8,8,8,512]{3,2,1,0:T(8,128)(2,1)} %tok_hbm.1) | copy-start | bytes 1572868
  4.0 1.0 %copy-start.2 = (bf16[3,512,128]{2,1,0:T(8,128)(2,1)S(1)}, bf16[3,512,128]{2,1,0:T(8,128)(2,1)}, u32[]{:S(2)}) copy-start(bf16[3,512,128]{2,1,0:T(8,128)(2,1)} %wc.1) | copy-start | bytes 1179652
  5.0 0.8 %copy-start.3 = (f32[3,4,1024]{2,1,0:T(4,128)S(1)}, f32[3,4,1024]{2,1,0:T(4,128)}, u32[]{:S(2)}) copy-start(f32[3,4,1024]{2,1,0:T(4,128)} %cv.1) | copy-start | bytes 147460
  5.8 0.7 %copy-start.4 = (f32[3,1024]{1,0:T(4,128)S(1)}, f32[3,1024]{1,0:T(4,128)}, u32[]{:S(2)}) copy-start(f32[3,1024]{1,0:T(4,128)} %og.1) | copy-start | bytes 36868
  6.5 0.7 %copy-start.5 = (f32[3,512]{1,0:T(4,128)S(1)}, f32[3,512]{1,0:T(4,128)}, u32[]{:S(2)}) copy-start(f32[3,512]{1,0:T(4,128)} %ng.1) | copy-start | bytes 18436
  7.2 0.7 %copy-start.6 = (f32[3,4,128]{2,1,0:T(4,128)S(1)}, f32[3,4,128]{2,1,0:T(4,128)}, u32[]{:S(2)}) copy-start(f32[3,4,128]{2,1,0:T(4,128)} %cc.1) | copy-start | bytes 18436
  7.9 0.7 %copy-start.7 = (f32[3,16]{1,0:T(4,128)S(1)}, f32[3,16]{1,0:T(4,128)}, u32[]{:S(2)}) copy-start(f32[3,16]{1,0:T(4,128)} %sb.1) | copy-start | bytes 580
  8.5 0.7 %copy-start.8 = (f32[3,16]{1,0:T(4,128)S(1)}, f32[3,16]{1,0:T(4,128)}, u32[]{:S(2)}) copy-start(f32[3,16]{1,0:T(4,128)} %rl.1) | copy-start | bytes 580
  9.2 0.7 %copy-start.9 = (f32[3,16]{1,0:T(4,128)S(1)}, f32[3,16]{1,0:T(4,128)}, u32[]{:S(2)}) copy-start(f32[3,16]{1,0:T(4,128)} %sk.1) | copy-start | bytes 580
where the time goes:
time: 49.9 us; the launch traced here: 49.3 us
  Pallas kernels  38.6 us (77%)
  local copies, waits for them, and re-layouts  10.7 us (21%)
    pallas_call x1, Pallas kernels, shards(): pl.pallas_call(functools.partial(sweeps, sizes), out_shape=jax.ShapeDtype...  38.6 us
    unnamed x22, local copies, waits for them, and re-layouts  10.7 us

commit v1 on v0

--- a/solution.py
+++ b/solution.py
@@ -157,7 +157,9 @@
     scale = lax.rsqrt(jnp.mean(x * x, axis=-1, keepdims=True) + 1e-05)
     normed = (x * scale * ng[layer : layer + 1, :]).astype(BF16)
     coupling = rounded(jnp.dot(normed, wc[layer], preferred_element_type=F32))
-    steps = jnp.dot(normed, ws[layer], preferred_element_type=F32)
+    steps = lax.dot_general(
+        normed, ws[layer], (((1,), (1,)), ((), ())), preferred_element_type=F32
+    )
     store(None, (coupling, steps))
     total = wg.shape[2]
     for first in range(0, total, n_block):
@@ -248,10 +250,10 @@
 
 
 def sweeps(
-    sizes, tok_hbm, ng, wg_hbm, wc, ws, cv, cc, sb, rl, sk, og, wo_hbm, out,
-    tok, wg, wo, x0, gv0, coup0, step0, gv1, x2, gv2, coup2, step2,
+    sizes, tok_hbm, ng_hbm, wg_hbm, wc_hbm, ws_hbm, cv_hbm, cc_hbm, sb_hbm, rl_hbm, sk_hbm,
+    og_hbm, wo_hbm, out, tok, ng, wg, wc, ws, cv, cc, sb, rl, sk, og, wo, x0, gv0, coup0, step0, gv1, x2, gv2, coup2, step2,
     landed, sent, gated, normal, back,
-    tok_sem, wg_sem, wo_sem, send1, recv1, send2, recv2,
+    tok_sem, small_sem, wg_sem, wo_sem, send1, recv1, send2, recv2,
 ):
     ha_n, wa_n, frames, rows_dev, cols_dev, width = sizes
     peers = ha_n * wa_n
@@ -269,6 +271,16 @@
 
     fetch = pltpu.make_async_copy(tok_hbm, tok, tok_sem)
     fetch.start()
+    small = []
+    for n, (src, dst) in enumerate(
+        (
+            (ng_hbm, ng), (wc_hbm, wc), (ws_hbm, ws), (cv_hbm, cv), (cc_hbm, cc),
+            (sb_hbm, sb), (rl_hbm, rl), (sk_hbm, sk), (og_hbm, og),
+        )
+    ):
+        copy = pltpu.make_async_copy(src, dst, small_sem.at[n])
+        copy.start()
+        small.append(copy)
     wg_copies = {}
     wo_copies = []
     layers = wg.shape[0]
@@ -295,6 +307,8 @@
     inner = cv.shape[2]
 
     fetch.wait()
+    for copy in small:
+        copy.wait()
     swap = swap_matrix(ROWS // (rows_dev * cols_dev), cols_dev, rows_dev)
     for first in range(0, tokens, ROWS):
         part = tok[...].astype(F32).reshape(tokens, width)[first : first + ROWS].astype(BF16)
@@ -456,6 +470,7 @@
     ha_n, wa_n = lax.axis_size("ha"), lax.axis_size("wa")
     if not fits(tokens, ha_n, wa_n):
         return shards_general(*arrays)
+    ws = ws.transpose(0, 2, 1)
     frames, rows_dev, cols_dev, width = tokens.shape
     count = frames * rows_dev * cols_dev
     layers, _, wide = wg.shape
@@ -472,27 +487,27 @@
     return pl.pallas_call(
         functools.partial(sweeps, sizes),
         out_shape=jax.ShapeDtypeStruct(tokens.shape, BF16),
-        in_specs=[hbm, vmem, hbm, vmem, vmem, vmem, vmem, vmem, vmem, vmem, vmem, hbm],
+        in_specs=[hbm] * 12,
         out_specs=vmem,
         scratch_shapes=[
             pltpu.VMEM(tokens.shape, BF16),
-            pltpu.VMEM(wg.shape, BF16),
-            pltpu.VMEM(wo.shape, BF16),
+            *(pltpu.VMEM(a.shape, a.dtype) for a in (ng, wg, wc, ws, cv, cc, sb, rl, sk, og, wo)),
             pltpu.VMEM(early + (width,), F32),
             pltpu.VMEM(early + (wide,), F32),
             pltpu.VMEM(early + (wc.shape[2],), F32),
-            pltpu.VMEM(early + (ws.shape[2],), F32),
+            pltpu.VMEM(early + (ws.shape[1],), F32),
             pltpu.VMEM((ROWS, wide), F32),
             pltpu.VMEM(late + (width,), F32),
             pltpu.VMEM(late + (wide,), F32),
             pltpu.VMEM(late + (wc.shape[2],), F32),
-            pltpu.VMEM(late + (ws.shape[2],), F32),
+            pltpu.VMEM(late + (ws.shape[1],), F32),
             pltpu.VMEM((chunks, wa_n, cpc, ha_n, rows_dev, width), BF16),
             pltpu.VMEM((frames, chunks, cpc, rows_dev, width), BF16),
             pltpu.VMEM((ROWS, inner), F32),
             pltpu.VMEM((ROWS, inner), BF16),
             pltpu.VMEM((ha_n, wa_n, rows_dev, cols_dev, width), BF16),
             dma(()),
+            dma((9,)),
             dma((layers, blocks)),
             dma((layers,)),
             dma((chunks, ha_n * wa_n)),
@@ -501,7 +516,7 @@
             dma((ha_n, wa_n)),
         ],
         compiler_params=pltpu.CompilerParams(
-            collective_id=0, has_side_effects=True, vmem_limit_bytes=48 * 2**20
+            collective_id=0, has_side_effects=True, vmem_limit_bytes=67043328
         ),
     )(tokens, ng, wg, wc, ws, cv, cc, sb, rl, sk, og, wo)
 

time: 49.9 us -> 44.7 us (0.90)
  local copies, waits for them, and re-layouts: 10.7 us -> 1.87 us
  Pallas kernels: 38.6 us -> 42.6 us
    unnamed x22 -> x1, local copies, waits for them, and re-layouts: 10.7 us -> 1.87 us
    pallas_call x1, Pallas kernels: 38.6 us -> 42.6 us  [shards(): pl.pallas_call(functools.partial(sweeps, sizes), out_shape=jax.ShapeDtype...]
where the time goes in v1:
time: 44.7 us; the launch traced here: 44.5 us
  Pallas kernels  42.6 us (95%)
  local copies, waits for them, and re-layouts  1.87 us (4%)
    pallas_call x1, Pallas kernels, shards(): pl.pallas_call(functools.partial(sweeps, sizes), out_shape=jax.ShapeDtype...  42.6 us
    unnamed x1, local copies, waits for them, and re-layouts  1.87 us

profile of v1, /device:TPU:0, one launch (start us, length us, event | category | flops | bytes accessed | tf_op | source)
XLA Modules:
  0.0 44.5 jit_solution(12286644426884892860)
XLA Ops:
  0.0 42.6 %shard_map.118 = bf16[8,8,8,512]{3,2,1,0:T(8,128)(2,1)} custom-call(bf16[8,8,8,512]{3,2,1,0:T(8,128)(2,1)} %tok_hbm.1, f32[3,512]{1,0:T(4,128)} %ng_hbm.1, bf16[3,512,2048]{2,1,0:T(8,128)(2,1)} %wg_hbm.1, bf16[3,512,128]{2,1,0:T(8,128)(2,1)} %wc_hbm.1, bf16[3,16,512]{2,1,0:T(8,128)(2,1)} %bitcast.1, f32[3,4,1024]{2,1,0:T(4,128)} %cv_hbm.1, ...), custom_call_target="tpu_custom_call" | custom-call | tf_op jit(solution)/shard_map/pallas_call | solution.py:487
  42.6 1.9 %copy.14 = bf16[8,8,8,512]{3,2,1,0:T(8,128)(2,1)} copy(bf16[8,8,8,512]{3,2,1,0:T(8,128)(2,1)} %shard_map.118) | data formatting | bytes 1048576

commit v2 on v1

--- a/solution.py
+++ b/solution.py
@@ -143,8 +143,10 @@
 MESH = pl.DeviceIdType.MESH
 
 
-def silu(x):
-    half = 0.5 * x
+LOG2E = 1.4426950408889634
+
+
+def silu_of_half(half):
     return half + half * jnp.tanh(half)
 
 
@@ -152,31 +154,61 @@
     return x.astype(BF16).astype(F32)
 
 
-def project(layer, x, refs, n_block, store, wait=None):
-    wg, wc, ws, ng = refs
+def project(layer, length, stride, x, refs, n_block, emit, wait=None):
+    wg, wc, ws, ng, cv, cc, sb, rl = refs
+    rows = x.shape[0]
+    inner = cv.shape[2]
+    taps = cv.shape[1]
+
+    def shift(v, by):
+        if stride == 1:
+            position = lax.broadcasted_iota(jnp.int32, v.shape, 0) % length
+            return jnp.where(position >= by, pltpu.roll(v, by, 0), 0.0)
+        pad = jnp.zeros((by * stride, v.shape[1]), v.dtype)
+        return jnp.concatenate([pad, v[: rows - by * stride]], axis=0)
+
+    def conv(v, kernel):
+        half = 0.5 * kernel
+        total = v * half[taps - 1 : taps]
+        for back in range(1, taps):
+            total = total + shift(v, back) * half[taps - 1 - back : taps - back]
+        return rounded(silu_of_half(total))
+
     scale = lax.rsqrt(jnp.mean(x * x, axis=-1, keepdims=True) + 1e-05)
     normed = (x * scale * ng[layer : layer + 1, :]).astype(BF16)
     coupling = rounded(jnp.dot(normed, wc[layer], preferred_element_type=F32))
-    steps = lax.dot_general(
-        normed, ws[layer], (((1,), (1,)), ((), ())), preferred_element_type=F32
-    )
-    store(None, (coupling, steps))
-    total = wg.shape[2]
-    for first in range(0, total, n_block):
+    emit("maps", 0, conv(coupling, cc[layer]))
+    raw = lax.dot_general(normed, ws[layer], (((1,), (1,)), ((), ())), preferred_element_type=F32)
+    raw = raw + sb[layer : layer + 1, :]
+    steps = jnp.maximum(raw, 0.0) + jnp.log1p(jnp.exp(-jnp.abs(raw)))
+    cumul = steps * -jnp.exp(rl[layer : layer + 1, :])
+    by = 1
+    while by < length:
+        cumul = cumul + shift(cumul, by)
+        by *= 2
+    cumul = cumul * LOG2E
+    emit("decay", 0, cumul)
+    emit("source", 0, cumul - jnp.log(steps) * LOG2E)
+    for first in range(0, 2 * inner, n_block):
         if wait is not None:
-            wait(first // n_block)
-        block = jnp.dot(normed, wg[layer, :, first : first + n_block], preferred_element_type=F32)
-        store(first, rounded(block))
-
-
-def mix(layer, length, stride, gate_of, value_of, coupling, steps, x, params, gated, normal):
-    cv, cc, sb, rl, sk, og, wo = params
-    rows = coupling.shape[0]
-    heads = sb.shape[1]
-    inner = cv.shape[2]
+            wait(first)
+        block = rounded(
+            jnp.dot(normed, wg[layer, :, first : first + n_block], preferred_element_type=F32)
+        )
+        if first < inner:
+            emit("gate", first, silu_of_half(0.5 * block))
+        else:
+            at = first - inner
+            emit("xs", at, conv(block, cv[layer, :, at : at + n_block]))
+
+
+def mix(layer, length, stride, read, x, params, gated, normal):
+    sk, og, wo = params
+    maps, decay_to, source = read("maps"), read("decay"), read("source")
+    rows, heads = decay_to.shape
+    inner = og.shape[1]
     headdim = inner // heads
-    taps = cv.shape[1]
-    states = coupling.shape[1] // 2
+    states = maps.shape[1] // 2
     i = lax.broadcasted_iota(jnp.int32, (rows, rows), 0)
     j = lax.broadcasted_iota(jnp.int32, (rows, rows), 1)
     if stride == 1:
@@ -184,44 +216,22 @@
     else:
         same = (i % stride) == (j % stride)
     mask = same & (i >= j)
-
-    def shift(v, by):
-        if stride == 1:
-            position = lax.broadcasted_iota(jnp.int32, v.shape, 0) % length
-            return jnp.where(position >= by, pltpu.roll(v, by, 0), 0.0)
-        pad = jnp.zeros((by * stride, v.shape[1]), v.dtype)
-        return jnp.concatenate([pad, v[: rows - by * stride]], axis=0)
-
-    def conv(v, kernel):
-        total = v * kernel[taps - 1 : taps]
-        for back in range(1, taps):
-            total = total + shift(v, back) * kernel[taps - 1 - back : taps - back]
-        return silu(total)
-
-    maps = conv(coupling, cc[layer]).astype(BF16)
+    maps = maps.astype(BF16)
     scores = lax.dot_general(
         maps[:, states:], maps[:, :states], (((1,), (1,)), ((), ())), preferred_element_type=F32
     )
-    raw = steps + sb[layer : layer + 1, :]
-    steps = jnp.maximum(raw, 0.0) + jnp.log1p(jnp.exp(-jnp.abs(raw)))
-    cumul = steps * -jnp.exp(rl[layer : layer + 1, :])
-    by = 1
-    while by < length:
-        cumul = cumul + shift(cumul, by)
-        by *= 2
-    cumul_t = cumul.T
-    steps_t = steps.T
+    source_t = source.T
     pair = 2 * headdim
     lane = lax.broadcasted_iota(jnp.int32, (1, pair), 1)
     squares = jnp.zeros((rows, pair), F32)
     for p in range(heads // 2):
         lanes = slice(p * pair, (p + 1) * pair)
-        xs = conv(value_of(lanes), cv[layer, :, lanes]).astype(BF16).astype(F32)
+        xs = read("xs", lanes)
         weights = []
         for h in (2 * p, 2 * p + 1):
-            spread = cumul[:, h : h + 1] - cumul_t[h : h + 1, :]
-            decay = jnp.exp(jnp.where(mask, spread, -jnp.inf))
-            weights.append((scores * decay * steps_t[h : h + 1, :]).astype(BF16))
+            spread = decay_to[:, h : h + 1] - source_t[h : h + 1, :]
+            decay = jnp.exp2(jnp.where(mask, spread, -jnp.inf))
+            weights.append((scores * decay).astype(BF16))
         both = jnp.concatenate(
             [jnp.where(lane < headdim, xs, 0.0), jnp.where(lane < headdim, 0.0, xs)], axis=0
         ).astype(BF16)
@@ -231,7 +241,7 @@
             sk[layer : layer + 1, 2 * p : 2 * p + 1],
             sk[layer : layer + 1, 2 * p + 1 : 2 * p + 2],
         )
-        part = (mixed + skip * xs) * silu(gate_of(lanes))
+        part = (mixed + skip * xs) * read("gate", lanes)
         squares = squares + part * part
         gated[:, lanes] = part
     scale = lax.rsqrt(jnp.sum(squares, axis=-1, keepdims=True) / inner + 1e-05)
@@ -251,11 +261,13 @@
 
 def sweeps(
     sizes, tok_hbm, ng_hbm, wg_hbm, wc_hbm, ws_hbm, cv_hbm, cc_hbm, sb_hbm, rl_hbm, sk_hbm,
-    og_hbm, wo_hbm, out, tok, ng, wg, wc, ws, cv, cc, sb, rl, sk, og, wo, x0, gv0, coup0, step0, gv1, x2, gv2, coup2, step2,
+    og_hbm, wo_hbm, out, tok, ng, wg, wc, ws, cv, cc, sb, rl, sk, og, wo, x0, x2,
+    gate0, xs0, maps0, decay0, source0, gate1, xs1, maps1, decay1, source1,
+    gate2, xs2, maps2, decay2, source2,
     landed, sent, gated, normal, back,
     tok_sem, small_sem, wg_sem, wo_sem, send1, recv1, send2, recv2,
 ):
-    ha_n, wa_n, frames, rows_dev, cols_dev, width = sizes
+    ha_n, wa_n, frames, rows_dev, cols_dev, width, group1 = sizes
     peers = ha_n * wa_n
     cpc = ROWS // (frames * rows_dev)
     chunks = cols_dev // cpc
@@ -265,6 +277,7 @@
     me = ha * wa_n + wa
     blocks = wg_sem.shape[1]
     n_block = wg.shape[2] // blocks
+    n_dot = n_block // 2
 
     def device(index):
         return {"ha": index // wa_n, "wa": lax.rem(index, wa_n)}
@@ -302,9 +315,12 @@
             barrier, inc=1, device_id=device(lax.rem(me + k, peers)), device_id_type=MESH
         )
 
-    refs = (wg, wc, ws, ng)
-    params = (cv, cc, sb, rl, sk, og, wo)
-    inner = cv.shape[2]
+    refs = (wg, wc, ws, ng, cv, cc, sb, rl)
+    params = (sk, og, wo)
+    names = ("gate", "xs", "maps", "decay", "source")
+    kept0 = dict(zip(names, (gate0, xs0, maps0, decay0, source0)))
+    kept1 = dict(zip(names, (gate1, xs1, maps1, decay1, source1)))
+    kept2 = dict(zip(names, (gate2, xs2, maps2, decay2, source2)))
 
     fetch.wait()
     for copy in small:
@@ -317,30 +333,30 @@
             swap, part, preferred_element_type=F32
         ).reshape(group, rows_dev * cols_dev, width)
 
-    def keep_in(wide, coupling, steps):
-        def store(first, value):
-            if first is None:
-                coupling[...] = value[0].reshape(coupling.shape)
-                steps[...] = value[1].reshape(steps.shape)
-            else:
-                size = value.shape[1]
-                wide[:, :, first : first + size] = value.reshape(wide.shape[:2] + (size,))
-
-        return store
+    def keep_in(kept):
+        def emit(name, first, value):
+            ref = kept[name]
+            size = value.shape[1]
+            ref[:, :, first : first + size] = value.reshape(ref.shape[:2] + (size,))
+
+        return emit
+
+    def wait0(first):
+        if first % n_block == 0:
+            wg_copies[0, first // n_block].wait()
 
     project(
-        0, x0[...].reshape(tokens, width), refs, n_block, keep_in(gv0, coup0, step0),
-        lambda b: wg_copies[0, b].wait(),
+        0, frames, rows_dev * cols_dev, x0[...].reshape(tokens, width), refs, n_dot,
+        keep_in(kept0), wait0,
     )
     wo_copies[0].wait()
     pl.semaphore_wait(barrier, peers - 1)
 
     span = rows_dev * cpc
 
-    def view(ref, c, size):
-        return lambda lanes: ref[
-            :, pl.ds(pl.multiple_of(c * size, size), size), lanes
-        ].reshape(ROWS, -1)
+    def view(kept, c, size):
+        part = pl.ds(pl.multiple_of(c * size, size), size)
+        return lambda name, lanes=slice(None): kept[name][:, part, lanes].reshape(ROWS, -1)
 
     def out1(c, k):
         peer = lax.rem(me + k, peers)
@@ -354,13 +370,8 @@
         )
 
     def layer0(c, carry):
-        pick = view(gv0, c, span)
         y = mix(
-            0, frames, span,
-            lambda lanes: pick(lanes),
-            lambda lanes: pick(slice(inner + lanes.start, inner + lanes.stop)),
-            view(coup0, c, span)(slice(None)), view(step0, c, span)(slice(None)),
-            view(x0, c, span)(slice(None)),
+            0, frames, span, view(kept0, c, span), view({"x": x0}, c, span)("x"),
             params, gated, normal,
         )
         sent[:, pl.ds(c, 1)] = y.reshape(frames, 1, cpc, rows_dev, width).astype(BF16)
@@ -377,36 +388,39 @@
         wg_copies[1, b].wait()
     wo_copies[1].wait()
 
-    def layer1(c, carry):
-        for k in range(1, peers):
-            out1(c, k).wait_recv()
+    def layer1(half, carry):
+        for part in range(group1):
+            for k in range(1, peers):
+                out1(half * group1 + part, k).wait_recv()
+        x = landed[pl.ds(half * group1, group1)].astype(F32).reshape(group1 * ROWS, width)
+
+        def emit(name, first, value):
+            kept1[name][:, first : first + value.shape[1]] = value
+
+        project(1, rows_all, 1, x, refs, n_dot, emit)
+        for part in range(group1):
+            layer1_mix(half * group1 + part, part * ROWS)
+        return carry
+
+    def layer1_mix(c, first):
         x = landed[pl.ds(c, 1)].astype(F32).reshape(ROWS, width)
-        held = []
-
-        def store_part(first, value):
-            if first is None:
-                held.extend(value)
-            else:
-                gv1[:, first : first + value.shape[1]] = value
-
-        project(1, x, refs, n_block, store_part)
         y = mix(
             1, rows_all, 1,
-            lambda lanes: gv1[:, lanes],
-            lambda lanes: gv1[:, inner + lanes.start : inner + lanes.stop],
-            held[0], held[1], x, params, gated, normal,
+            lambda name, lanes=slice(None): kept1[name][first : first + ROWS, lanes],
+            x, params, gated, normal,
         )
         y = rounded(y).reshape(wa_n, cpc, rows_all, width)
         for w in range(wa_n):
             x2[pl.ds(w * cols_dev + c * cpc, cpc)] = y[w]
-        return carry
-
-    lax.fori_loop(0, chunks, layer1, 0)
+
+    lax.fori_loop(0, chunks // group1, layer1, 0)
 
     for b in range(blocks):
         wg_copies[2, b].wait()
     wo_copies[2].wait()
-    project(2, x2[...].reshape(tokens, width), refs, n_block, keep_in(gv2, coup2, step2))
+    project(
+        2, cols_all, rows_all, x2[...].reshape(tokens, width), refs, n_dot, keep_in(kept2)
+    )
     swap2 = swap_matrix(wa_n, rows_dev, cols_dev)
 
     def out2(j, q):
@@ -422,13 +436,8 @@
 
     def layer2(j, carry):
         c = lax.rem(ha + j + 1, ha_n)
-        pick = view(gv2, c, rows_dev)
         y = mix(
-            2, cols_all, rows_dev,
-            lambda lanes: pick(lanes),
-            lambda lanes: pick(slice(inner + lanes.start, inner + lanes.stop)),
-            view(coup2, c, rows_dev)(slice(None)), view(step2, c, rows_dev)(slice(None)),
-            view(x2, c, rows_dev)(slice(None)),
+            2, cols_all, rows_dev, view(kept2, c, rows_dev), view({"x": x2}, c, rows_dev)("x"),
             params, gated, normal,
         )
         turned = jnp.dot(swap2, y.astype(BF16), preferred_element_type=F32)
@@ -478,11 +487,12 @@
     cpc = ROWS // (frames * rows_dev)
     chunks = cols_dev // cpc
     blocks = 4
+    group1 = 2 if chunks % 2 == 0 else 1
     early = (frames, rows_dev * cols_dev)
     late = (cols_dev * wa_n, rows_dev * ha_n)
     vmem = pl.BlockSpec(memory_space=pltpu.VMEM)
     hbm = pl.BlockSpec(memory_space=pl.ANY)
-    sizes = (ha_n, wa_n, frames, rows_dev, cols_dev, width)
+    sizes = (ha_n, wa_n, frames, rows_dev, cols_dev, width, group1)
     dma = pltpu.SemaphoreType.DMA
     return pl.pallas_call(
         functools.partial(sweeps, sizes),
@@ -493,14 +503,12 @@
             pltpu.VMEM(tokens.shape, BF16),
             *(pltpu.VMEM(a.shape, a.dtype) for a in (ng, wg, wc, ws, cv, cc, sb, rl, sk, og, wo)),
             pltpu.VMEM(early + (width,), F32),
-            pltpu.VMEM(early + (wide,), F32),
-            pltpu.VMEM(early + (wc.shape[2],), F32),
-            pltpu.VMEM(early + (ws.shape[1],), F32),
-            pltpu.VMEM((ROWS, wide), F32),
             pltpu.VMEM(late + (width,), F32),
-            pltpu.VMEM(late + (wide,), F32),
-            pltpu.VMEM(late + (wc.shape[2],), F32),
-            pltpu.VMEM(late + (ws.shape[1],), F32),
+            *(
+                pltpu.VMEM(lead + (size,), F32)
+                for lead in (early, (group1 * ROWS,), late)
+                for size in (inner, inner, wc.shape[2], ws.shape[1], ws.shape[1])
+            ),
             pltpu.VMEM((chunks, wa_n, cpc, ha_n, rows_dev, width), BF16),
             pltpu.VMEM((frames, chunks, cpc, rows_dev, width), BF16),
             pltpu.VMEM((ROWS, inner), F32),

time: 44.7 us -> 46.4 us (1.038)
  Pallas kernels: 42.6 us -> 44.4 us
    pallas_call x1, Pallas kernels: 42.6 us -> 44.4 us  [shards(): pl.pallas_call(functools.partial(sweeps, sizes), out_shape=jax.ShapeDtype...]
where the time goes in v2:
time: 46.4 us; the launch traced here: 46.3 us
  Pallas kernels  44.4 us (96%)
  local copies, waits for them, and re-layouts  1.87 us (4%)
    pallas_call x1, Pallas kernels, shards(): pl.pallas_call(functools.partial(sweeps, sizes), out_shape=jax.ShapeDtype...  44.4 us
    unnamed x1, local copies, waits for them, and re-layouts  1.87 us

profile of v2, /device:TPU:0, one launch (start us, length us, event | category | flops | bytes accessed | tf_op | source)
XLA Modules:
  0.0 46.3 jit_solution(4815279746908571655)
XLA Ops:
  0.0 44.4 %shard_map.118 = bf16[8,8,8,512]{3,2,1,0:T(8,128)(2,1)} custom-call(bf16[8,8,8,512]{3,2,1,0:T(8,128)(2,1)} %tok_hbm.1, f32[3,512]{1,0:T(4,128)} %ng_hbm.1, bf16[3,512,2048]{2,1,0:T(8,128)(2,1)} %wg_hbm.1, bf16[3,512,128]{2,1,0:T(8,128)(2,1)} %wc_hbm.1, bf16[3,16,512]{2,1,0:T(8,128)(2,1)} %bitcast.1, f32[3,4,1024]{2,1,0:T(4,128)} %cv_hbm.1, ...), custom_call_target="tpu_custom_call" | custom-call | tf_op jit(solution)/shard_map/pallas_call | solution.py:497
  44.4 1.9 %copy.14 = bf16[8,8,8,512]{3,2,1,0:T(8,128)(2,1)} copy(bf16[8,8,8,512]{3,2,1,0:T(8,128)(2,1)} %shard_map.118) | data formatting | bytes 1048576

commit v3 on v2

--- a/solution.py
+++ b/solution.py
@@ -262,12 +262,11 @@
 def sweeps(
     sizes, tok_hbm, ng_hbm, wg_hbm, wc_hbm, ws_hbm, cv_hbm, cc_hbm, sb_hbm, rl_hbm, sk_hbm,
     og_hbm, wo_hbm, out, tok, ng, wg, wc, ws, cv, cc, sb, rl, sk, og, wo, x0, x2,
-    gate0, xs0, maps0, decay0, source0, gate1, xs1, maps1, decay1, source1,
-    gate2, xs2, maps2, decay2, source2,
+    gate, xs, maps, decay, source,
     landed, sent, gated, normal, back,
     tok_sem, small_sem, wg_sem, wo_sem, send1, recv1, send2, recv2,
 ):
-    ha_n, wa_n, frames, rows_dev, cols_dev, width, group1 = sizes
+    ha_n, wa_n, frames, rows_dev, cols_dev, width = sizes
     peers = ha_n * wa_n
     cpc = ROWS // (frames * rows_dev)
     chunks = cols_dev // cpc
@@ -297,7 +296,8 @@
     wg_copies = {}
     wo_copies = []
     layers = wg.shape[0]
-    for layer in range(layers):
+
+    def start_weights(layer):
         for b in range(blocks):
             span = pl.ds(b * n_block, n_block)
             copy = pltpu.make_async_copy(
@@ -309,6 +309,8 @@
         copy.start()
         wo_copies.append(copy)
 
+    start_weights(0)
+
     barrier = pltpu.get_barrier_semaphore()
     for k in range(1, peers):
         pl.semaphore_signal(
@@ -317,10 +319,17 @@
 
     refs = (wg, wc, ws, ng, cv, cc, sb, rl)
     params = (sk, og, wo)
-    names = ("gate", "xs", "maps", "decay", "source")
-    kept0 = dict(zip(names, (gate0, xs0, maps0, decay0, source0)))
-    kept1 = dict(zip(names, (gate1, xs1, maps1, decay1, source1)))
-    kept2 = dict(zip(names, (gate2, xs2, maps2, decay2, source2)))
+    kept = dict(gate=gate, xs=xs, maps=maps, decay=decay, source=source)
+
+    def emit(name, first, value):
+        kept[name][:, first : first + value.shape[1]] = value
+
+    def read(name, lanes=slice(None)):
+        return kept[name][:, lanes]
+
+    def run(layer, length, stride, x):
+        project(layer, length, stride, x, refs, n_dot, emit)
+        return mix(layer, length, stride, read, x, params, gated, normal)
 
     fetch.wait()
     for copy in small:
@@ -333,30 +342,17 @@
             swap, part, preferred_element_type=F32
         ).reshape(group, rows_dev * cols_dev, width)
 
-    def keep_in(kept):
-        def emit(name, first, value):
-            ref = kept[name]
-            size = value.shape[1]
-            ref[:, :, first : first + size] = value.reshape(ref.shape[:2] + (size,))
-
-        return emit
-
-    def wait0(first):
-        if first % n_block == 0:
-            wg_copies[0, first // n_block].wait()
-
-    project(
-        0, frames, rows_dev * cols_dev, x0[...].reshape(tokens, width), refs, n_dot,
-        keep_in(kept0), wait0,
-    )
+    for b in range(blocks):
+        wg_copies[0, b].wait()
     wo_copies[0].wait()
+    for layer in range(1, layers):
+        start_weights(layer)
     pl.semaphore_wait(barrier, peers - 1)
 
     span = rows_dev * cpc
 
-    def view(kept, c, size):
-        part = pl.ds(pl.multiple_of(c * size, size), size)
-        return lambda name, lanes=slice(None): kept[name][:, part, lanes].reshape(ROWS, -1)
+    def view(ref, c, size):
+        return ref[:, pl.ds(pl.multiple_of(c * size, size), size), :].reshape(ROWS, width)
 
     def out1(c, k):
         peer = lax.rem(me + k, peers)
@@ -370,10 +366,7 @@
         )
 
     def layer0(c, carry):
-        y = mix(
-            0, frames, span, view(kept0, c, span), view({"x": x0}, c, span)("x"),
-            params, gated, normal,
-        )
+        y = run(0, frames, span, view(x0, c, span))
         sent[:, pl.ds(c, 1)] = y.reshape(frames, 1, cpc, rows_dev, width).astype(BF16)
         for k in range(1, peers):
             out1(c, k).start()
@@ -388,43 +381,30 @@
         wg_copies[1, b].wait()
     wo_copies[1].wait()
 
-    def layer1(half, carry):
-        for part in range(group1):
-            for k in range(1, peers):
-                out1(half * group1 + part, k).wait_recv()
-        x = landed[pl.ds(half * group1, group1)].astype(F32).reshape(group1 * ROWS, width)
-
-        def emit(name, first, value):
-            kept1[name][:, first : first + value.shape[1]] = value
-
-        project(1, rows_all, 1, x, refs, n_dot, emit)
-        for part in range(group1):
-            layer1_mix(half * group1 + part, part * ROWS)
-        return carry
-
-    def layer1_mix(c, first):
-        x = landed[pl.ds(c, 1)].astype(F32).reshape(ROWS, width)
-        y = mix(
-            1, rows_all, 1,
-            lambda name, lanes=slice(None): kept1[name][first : first + ROWS, lanes],
-            x, params, gated, normal,
-        )
+    def layer1(c, carry):
+        for k in range(1, peers):
+            out1(c, k).wait_recv()
+        y = run(1, rows_all, 1, landed[pl.ds(c, 1)].astype(F32).reshape(ROWS, width))
         y = rounded(y).reshape(wa_n, cpc, rows_all, width)
         for w in range(wa_n):
             x2[pl.ds(w * cols_dev + c * cpc, cpc)] = y[w]
-
-    lax.fori_loop(0, chunks // group1, layer1, 0)
+        return carry
+
+    lax.fori_loop(0, chunks, layer1, 0)
 
     for b in range(blocks):
         wg_copies[2, b].wait()
     wo_copies[2].wait()
-    project(
-        2, cols_all, rows_all, x2[...].reshape(tokens, width), refs, n_dot, keep_in(kept2)
-    )
     swap2 = swap_matrix(wa_n, rows_dev, cols_dev)
 
+    def target(j):
+        if ha_n != 4:
+            return lax.rem(ha + j + 1, ha_n)
+        mirrored = ha + ((j + 1) // 2 % 2) * (ha_n - 1 - 2 * ha)
+        return lax.rem(mirrored + (1 - j % 2) * (ha_n // 2), ha_n)
+
     def out2(j, q):
-        peer_ha, peer_wa = lax.rem(ha + j + 1, ha_n), lax.rem(wa + q, wa_n)
+        peer_ha, peer_wa = target(j), lax.rem(wa + q, wa_n)
         return pltpu.make_async_remote_copy(
             src_ref=back.at[j, peer_wa],
             dst_ref=out.at[me],
@@ -435,11 +415,8 @@
         )
 
     def layer2(j, carry):
-        c = lax.rem(ha + j + 1, ha_n)
-        y = mix(
-            2, cols_all, rows_dev, view(kept2, c, rows_dev), view({"x": x2}, c, rows_dev)("x"),
-            params, gated, normal,
-        )
+        c = target(j)
+        y = run(2, cols_all, rows_dev, view(x2, c, rows_dev))
         turned = jnp.dot(swap2, y.astype(BF16), preferred_element_type=F32)
         back[pl.ds(j, 1)] = turned.reshape(1, wa_n, rows_dev, cols_dev, width).astype(BF16)
         for q in range(wa_n):
@@ -487,12 +464,11 @@
     cpc = ROWS // (frames * rows_dev)
     chunks = cols_dev // cpc
     blocks = 4
-    group1 = 2 if chunks % 2 == 0 else 1
     early = (frames, rows_dev * cols_dev)
     late = (cols_dev * wa_n, rows_dev * ha_n)
     vmem = pl.BlockSpec(memory_space=pltpu.VMEM)
     hbm = pl.BlockSpec(memory_space=pl.ANY)
-    sizes = (ha_n, wa_n, frames, rows_dev, cols_dev, width, group1)
+    sizes = (ha_n, wa_n, frames, rows_dev, cols_dev, width)
     dma = pltpu.SemaphoreType.DMA
     return pl.pallas_call(
         functools.partial(sweeps, sizes),
@@ -505,8 +481,7 @@
             pltpu.VMEM(early + (width,), F32),
             pltpu.VMEM(late + (width,), F32),
             *(
-                pltpu.VMEM(lead + (size,), F32)
-                for lead in (early, (group1 * ROWS,), late)
+                pltpu.VMEM((ROWS, size), F32)
                 for size in (inner, inner, wc.shape[2], ws.shape[1], ws.shape[1])
             ),
             pltpu.VMEM((chunks, wa_n, cpc, ha_n, rows_dev, width), BF16),

time: 46.4 us -> 39.6 us (0.85)
  Pallas kernels: 44.4 us -> 37.6 us
    pallas_call x1, Pallas kernels: 44.4 us -> 37.6 us  [shards(): pl.pallas_call(functools.partial(sweeps, sizes), out_shape=jax.ShapeDtype...]
where the time goes in v3:
time: 39.6 us; the launch traced here: 39.5 us
  Pallas kernels  37.6 us (95%)
  local copies, waits for them, and re-layouts  1.87 us (5%)
    pallas_call x1, Pallas kernels, shards(): pl.pallas_call(functools.partial(sweeps, sizes), out_shape=jax.ShapeDtype...  37.6 us
    unnamed x1, local copies, waits for them, and re-layouts  1.87 us

profile of v3, /device:TPU:0, one launch (start us, length us, event | category | flops | bytes accessed | tf_op | source)
XLA Modules:
  0.0 39.5 jit_solution(14210206483419404608)
XLA Ops:
  0.0 37.6 %shard_map.118 = bf16[8,8,8,512]{3,2,1,0:T(8,128)(2,1)} custom-call(bf16[8,8,8,512]{3,2,1,0:T(8,128)(2,1)} %tok_hbm.1, f32[3,512]{1,0:T(4,128)} %ng_hbm.1, bf16[3,512,2048]{2,1,0:T(8,128)(2,1)} %wg_hbm.1, bf16[3,512,128]{2,1,0:T(8,128)(2,1)} %wc_hbm.1, bf16[3,16,512]{2,1,0:T(8,128)(2,1)} %bitcast.1, f32[3,4,1024]{2,1,0:T(4,128)} %cv_hbm.1, ...), custom_call_target="tpu_custom_call" | custom-call | tf_op jit(solution)/shard_map/pallas_call | solution.py:473
  37.6 1.9 %copy.14 = bf16[8,8,8,512]{3,2,1,0:T(8,128)(2,1)} copy(bf16[8,8,8,512]{3,2,1,0:T(8,128)(2,1)} %shard_map.118) | data formatting | bytes 1048576

commit v4 on v3

--- a/solution.py
+++ b/solution.py
@@ -437,10 +437,15 @@
             out1(c, k).wait_send()
 
 
+def hand_on(src, dst):
+    dst[...] = src[...]
+
+
 def fits(tokens, ha_n, wa_n):
     frames, rows_dev, cols_dev, _ = tokens.shape
     return (
         frames == ha_n * wa_n
+        and frames % 2 == 0
         and rows_dev == 8
         and ROWS % (frames * rows_dev) == 0
         and cols_dev % (ROWS // (frames * rows_dev)) == 0
@@ -470,7 +475,7 @@
     hbm = pl.BlockSpec(memory_space=pl.ANY)
     sizes = (ha_n, wa_n, frames, rows_dev, cols_dev, width)
     dma = pltpu.SemaphoreType.DMA
-    return pl.pallas_call(
+    result = pl.pallas_call(
         functools.partial(sweeps, sizes),
         out_shape=jax.ShapeDtypeStruct(tokens.shape, BF16),
         in_specs=[hbm] * 12,
@@ -502,6 +507,15 @@
             collective_id=0, has_side_effects=True, vmem_limit_bytes=67043328
         ),
     )(tokens, ng, wg, wc, ws, cv, cc, sb, rl, sk, og, wo)
+    half = (frames // 2,) + tokens.shape[1:]
+    block = pl.BlockSpec(half, lambda i: (i, 0, 0, 0))
+    return pl.pallas_call(
+        hand_on,
+        out_shape=jax.ShapeDtypeStruct(tokens.shape, BF16),
+        grid=(2,),
+        in_specs=[block],
+        out_specs=block,
+    )(result)
 
 
 def solution(mesh):

time: 39.6 us -> 39.5 us (level)
  local copies, waits for them, and re-layouts: 1.87 us -> 0 us
  Pallas kernels: 37.6 us -> 39.3 us
    unnamed x1 -> x0, local copies, waits for them, and re-layouts: 1.87 us -> none
    pallas_call x0 -> x1, Pallas kernels: none -> 1.77 us  [shards(): pl.pallas_call(hand_on, out_shape=jax.ShapeDtypeStruct(tokens.shape, BF16...]
where the time goes in v4:
time: 39.5 us; the launch traced here: 39.4 us
  Pallas kernels  39.3 us (99%)
    pallas_call x1, Pallas kernels, shards(): pl.pallas_call(functools.partial(sweeps, sizes), out_shape=jax.ShapeDtype...  37.6 us
    pallas_call x1, Pallas kernels, shards(): pl.pallas_call(hand_on, out_shape=jax.ShapeDtypeStruct(tokens.shape, BF16...  1.77 us

profile of v4, /device:TPU:0, one launch (start us, length us, event | category | flops | bytes accessed | tf_op | source)
XLA Modules:
  0.0 39.4 jit_solution(16945496389517623000)
XLA Ops:
  0.0 37.6 %shard_map.118.src = bf16[8,8,8,512]{3,2,1,0:T(8,128)(2,1)} custom-call(bf16[8,8,8,512]{3,2,1,0:T(8,128)(2,1)} %tok_hbm.1, f32[3,512]{1,0:T(4,128)} %ng_hbm.1, bf16[3,512,2048]{2,1,0:T(8,128)(2,1)} %wg_hbm.1, bf16[3,512,128]{2,1,0:T(8,128)(2,1)} %wc_hbm.1, bf16[3,16,512]{2,1,0:T(8,128)(2,1)} %bitcast.1, f32[3,4,1024]{2,1,0:T(4,128)} %cv_hbm.1, ...), custom_call_target="tpu_custom_call" | custom-call | tf_op jit(solution)/shard_map/pallas_call | solution.py:478
  37.6 1.8 %shard_map.119 = bf16[8,8,8,512]{3,2,1,0:T(8,128)(2,1)} custom-call(bf16[8,8,8,512]{3,2,1,0:T(8,128)(2,1)} %shard_map.118.src), custom_call_target="tpu_custom_call" | custom-call | tf_op jit(solution)/shard_map/pallas_call | solution.py:512
